TPU v7x, 256 devices: a whole 4x4x8 slice. The times are simulated.
256 devices in a mesh: pix: 8 (over z), ang: 32 (over y, x, core).
Axes of the slice: x: 4, y: 4, z: 8, core: 2. Of those that a mesh axis runs over, the one named last changes fastest.
Arguments:
- volume: float32 [256, 128, 128], P(('pix', 'ang')), may hold values from -6 to 6
- projector: float32 [40960, 128, 128], P(('pix', 'ang')), may hold values from -0.078125 to 0.078125
- tile_ids: int32 [40960], P(('pix', 'ang')), may hold values from 0 to 1023, as said below
- counts: int32 [1024, 128, 128], P('ang'), may hold values from 64 to 4095
- ray_counts: int32 [32, 8], P('ang'), may hold values from 1 to 4, 20 in all within a row
Outputs:
- updated: float32 [256, 128, 128], P(('pix', 'ang'))
Inputs may be any that keep to these rules, and one draw needn't show every extreme that they name: `tile_ids`: within each device's aligned block of 160 entries the values are distinct; value v names ray block v // 32 and pixel tile v % 32 of that device. `ray_counts`: each row sums to 20; the largest entry of every row is 4.
All inputs are finite; a program needn't handle non-finite values.
Results may differ from a plain program's by a relative error of at most 0.0001.
Values sent between devices are 32-bit elements; how exact they have to be, the bound alone decides.
A program may use at most 128 MiB of HBM per device.

v0:
```python
import jax
import jax.numpy as jnp
from jax import lax
from jax.sharding import PartitionSpec as P

blank_flux = 4096.0
step_size = 0.5


def weighting(summed, measured, live_mask):
    weights = jnp.where(live_mask, measured / blank_flux, 0.0)
    measured_data = jnp.where(live_mask, jnp.log(blank_flux / measured), 0.0)
    return weights * (summed - measured_data)


def shards(volume, projector, tile_ids, counts, ray_counts):
    highest = lax.Precision.HIGHEST
    pix_devices = lax.axis_size("pix")
    tile_count = tile_ids.shape[0]
    full_volume = lax.all_gather(volume, "ang", axis=0, tiled=True)
    pixel_tiles = full_volume.shape[0]
    ray_blocks = counts.shape[0]
    capacity = ray_blocks // pix_devices
    block_rows = tile_ids // pixel_tiles
    block_cols = tile_ids % pixel_tiles
    picked = jnp.take(full_volume, block_cols, axis=0)
    forward_product = jnp.einsum("ksq,krq->ksr", picked, projector, precision=highest)
    row_onehot = (block_rows[None, :] == jnp.arange(ray_blocks, dtype=jnp.int32)[:, None]).astype(
        jnp.float32
    )
    partial_value = jnp.dot(
        row_onehot,
        forward_product.reshape(tile_count, -1),
        precision=highest,
        preferred_element_type=jnp.float32,
    ).reshape(counts.shape)
    slot_index = jnp.arange(ray_blocks, dtype=jnp.int32)
    owner_match = (slot_index // capacity)[:, None] == jnp.arange(pix_devices, dtype=jnp.int32)[
        None, :
    ]
    slot_limit = jnp.sum(jnp.where(owner_match, ray_counts[0][None, :], 0), axis=1)
    live_flags = slot_index % capacity < slot_limit
    live_mask = live_flags[:, None, None]
    measured = counts.astype(jnp.float32)
    outgoing = partial_value.reshape((pix_devices, capacity) + counts.shape[1:])
    received = lax.all_to_all(outgoing, "pix", split_axis=0, concat_axis=0, tiled=True)
    summed = jnp.sum(received, axis=0)
    first_slot = lax.axis_index("pix") * capacity
    own_measured = lax.dynamic_slice_in_dim(measured, first_slot, capacity, 0)
    own_live = lax.dynamic_slice_in_dim(live_mask, first_slot, capacity, 0)
    own_residual = weighting(summed, own_measured, own_live)
    residual = lax.all_gather(own_residual, "pix", axis=0, tiled=True)
    back_rows = jnp.take(residual, block_rows, axis=0)
    back_product = jnp.einsum("ksr,krq->ksq", back_rows, projector, precision=highest).reshape(
        tile_count, -1
    )
    col_onehot = (block_cols[None, :] == jnp.arange(pixel_tiles, dtype=jnp.int32)[:, None]).astype(
        jnp.float32
    )
    product = jnp.dot(
        col_onehot, back_product, precision=highest, preferred_element_type=jnp.float32
    )
    gradient = lax.psum_scatter(
        product.reshape((volume.shape[0] * lax.axis_size("ang"),) + volume.shape[1:]),
        "ang",
        scatter_dimension=0,
        tiled=True,
    )
    return volume - step_size * gradient


def solution(mesh):
    placed = (
        P(("pix", "ang"), None, None),
        P(("pix", "ang"), None, None),
        P(("pix", "ang")),
        P("ang", None, None),
        P("ang", None),
    )
    return jax.shard_map(
        shards, mesh=mesh, in_specs=placed, out_specs=P(("pix", "ang"), None, None), check_vma=False
    )
```

profile of v0, /device:TPU:1, one launch (start us, length us, event | category | flops | bytes accessed | tf_op | source)
XLA Modules:
  0.0 339.9 jit_solution(8360122270949410973)
XLA Ops:
  6.5 0.7 all-gather.3.cloned.1.call-update
  7.3 0.7 compare_and_fusion
  8.0 54.7 %all-gather.3.cloned.1.call-done = f32[32,128,128]{2,1,0:T(8,128)} async-done(((f32[1,128,128]{2,1,0:T(8,128)}), f32[32,128,128]{2,1,0:T(8,128)}) %all-gather.3.cloned.1.call-update) | async-done | bytes 2097168 | tf_op jit(solution)/shard_map/all_gather | solution.py:20
  62.7 11.7 %gather_fusion = f32[160,128,128]{2,1,0:T(8,128)} fusion(f32[32,128,128]{2,1,0:T(8,128)} %all-gather.3.cloned.1.call-done, s32[1024]{0:T(1024)S(1)} %pad_clamp_fusion.1), kind=kCustom, calls=%fused_computation.clone | custom fusion | bytes 20972160 | tf_op jit(solution)/shard_map/jit(_take)/gather | solution.py:26
  74.4 24.8 %fusion.7 = f32[160,128,128]{2,1,0:T(8,128)S(1)} fusion(f32[160,128,128]{2,1,0:T(8,128)} %param.8, f32[160,128,128]{2,1,0:T(8,128)} %gather_fusion, pred[160]{0:T(512)(128)(4,1)S(1)} %get-tuple-element.10), kind=kOutput, calls=%fused_computation.12 | convolution fusion | flops 4029153280 | bytes 31457440 | tf_op jit(solution)/shard_map/ksq,krq->ksr/dot_general | solution.py:27
  99.2 14.2 %fusion.3 = f32[8,4,128,128]{3,1,2,0:T(4,128)} fusion(s32[8,4]{1,0:T(8,128)S(1)} %multiply_add_fusion, s32[160]{0:T(256)S(1)} %get-tuple-element.7, f32[20,8,128,128]{3,2,1,0:T(8,128)S(1)} %bitcast.40), kind=kOutput, calls=%fused_computation.8 | convolution fusion | flops 1006638080 | bytes 12583680 | tf_op jit(solution)/shard_map/dot_general | solution.py:31
  113.4 6.7 %all-to-all-start = ((f32[8,4,128,128]{3,1,2,0:T(4,128)}), f32[8,4,128,128]{3,1,2,0:T(4,128)}, u32[]{:S(2)}, u32[]{:S(2)}) async-start(f32[8,4,128,128]{3,1,2,0:T(4,128)} %fusion.3), calls=%async_computation | async-start | bytes 4194304 | tf_op jit(solution)/shard_map/all_to_all | solution.py:46
  120.1 0.0 all-gather.5.cloned.1.call-start
  120.2 0.1 select_reduce_fusion
  120.3 0.1 dynamic_slice.6
  120.4 51.5 %all-to-all-done = f32[8,4,128,128]{3,1,2,0:T(4,128)} async-done(((f32[8,4,128,128]{3,1,2,0:T(4,128)}), f32[8,4,128,128]{3,1,2,0:T(4,128)}, u32[]{:S(2)}, u32[]{:S(2)}) %all-to-all-start) | async-done | bytes 2097184 | tf_op jit(solution)/shard_map/all_to_all | solution.py:46
  171.9 2.0 reduce_sum.19
  173.9 0.3 subtract_multiply_fusion
  174.1 0.7 copy.21
  174.9 0.0 all-gather.5.cloned.1.call-update
  174.9 0.0 reduce-scatter.2.cloned.1.call-start
  175.0 30.8 %all-gather.5.cloned.1.call-done = f32[32,128,128]{2,1,0:T(8,128)} async-done(((f32[4,128,128]{2,1,0:T(8,128)}), f32[32,128,128]{2,1,0:T(8,128)}) %all-gather.5.cloned.1.call-update) | async-done | bytes 2097168 | tf_op jit(solution)/shard_map/all_gather | solution.py:52
  205.7 11.9 %gather_fusion.1 = f32[160,128,128]{2,1,0:T(8,128)} fusion(f32[32,128,128]{2,1,0:T(8,128)} %all-gather.5.cloned.1.call-done, s32[1024]{0:T(1024)S(1)} %pad_clamp_fusion), kind=kCustom, calls=%fused_computation.1.clone | custom fusion | bytes 20972160 | tf_op jit(solution)/shard_map/jit(_take)/gather | solution.py:53
  217.7 14.3 %fusion.5 = f32[160,128,128]{2,1,0:T(8,128)S(1)} fusion(f32[160,128,128]{2,1,0:T(8,128)} %param.8, f32[160,128,128]{2,1,0:T(8,128)} %gather_fusion.1, pred[160]{0:T(512)(128)(4,1)S(1)} %get-tuple-element.6), kind=kOutput, calls=%fused_computation.10 | convolution fusion | flops 4029153280 | bytes 31457440 | tf_op jit(solution)/shard_map/ksr,krq->ksq/dot_general | solution.py:54
  232.0 9.6 %fusion = f32[32,128,128]{2,0,1:T(8,128)S(1)} fusion(s32[160]{0:T(256)S(1)} %get-tuple-element.11, f32[20,8,128,128]{3,2,1,0:T(8,128)S(1)} %bitcast.41), kind=kOutput, calls=%fused_computation.4 | convolution fusion | flops 1006638080 | bytes 12583552 | tf_op jit(solution)/shard_map/dot_general | solution.py:60
  241.6 2.6 copy.23
  244.2 0.0 reduce-scatter.2.cloned.1.call-update
  244.2 87.7 %reduce-scatter.2.cloned.1.call-done = f32[1,128,128]{2,1,0:T(8,128)} async-done(((f32[32,128,128]{2,1,0:T(8,128)}), f32[1,128,128]{2,1,0:T(8,128)}) %reduce-scatter.2.cloned.1.call-update) | async-done | bytes 65552 | tf_op jit(solution)/shard_map/reduce_scatter | solution.py:63
  331.9 1.5 multiply_subtract_fusion
  (15 shorter events, 0.1 us)
Async XLA Ops:
  6.5 113.8 %copy-start = (s32[32,128,128]{2,1,0:T(8,128)S(1)}, s32[32,128,128]{2,1,0:T(8,128)}, u32[]{:S(2)}) copy-start(s32[32,128,128]{2,1,0:T(8,128)} %param.10) | copy-start | bytes 6291460
  6.5 56.1 %all-gather.3.cloned.1.call-start = ((), (), s32[]{:S(2)}) async-start(), calls=%async_computation.2 | async-start | bytes 2162688 | tf_op jit(solution)/shard_map/all_gather | solution.py:20
  99.2 21.0 %copy-start.2 = (s32[1,8]{1,0:T(1,128)S(1)}, s32[1,8]{1,0:T(1,128)}, u32[]{:S(2)}) copy-start(s32[1,8]{1,0:T(1,128)} %param.11) | copy-start | bytes 100
  113.4 58.5 %all-to-all-start = ((f32[8,4,128,128]{3,1,2,0:T(4,128)}), f32[8,4,128,128]{3,1,2,0:T(4,128)}, u32[]{:S(2)}, u32[]{:S(2)}) async-start(f32[8,4,128,128]{3,1,2,0:T(4,128)} %fusion.3), calls=%async_computation | async-start | bytes 4194304 | tf_op jit(solution)/shard_map/all_to_all | solution.py:46
  120.1 85.6 %all-gather.5.cloned.1.call-start = ((), (), s32[]{:S(2)}) async-start(), calls=%async_computation.3 | async-start | bytes 2359296 | tf_op jit(solution)/shard_map/all_gather | solution.py:52
  174.9 157.0 %reduce-scatter.2.cloned.1.call-start = ((), (), s32[]{:S(2)}) async-start(), calls=%async_computation.4 | async-start | bytes 2162688 | tf_op jit(solution)/shard_map/reduce_scatter | solution.py:63
  232.0 99.9 %copy-start.1 = (f32[1,128,128]{2,1,0:T(8,128)S(1)}, f32[1,128,128]{2,1,0:T(8,128)}, u32[]{:S(2)}) copy-start(f32[1,128,128]{2,1,0:T(8,128)} %param.7) | copy-start | bytes 196612
Sparse Core Ops, SparseCore 0:
  9.9 52.7 all-gather.2
  175.0 30.6 all-gather.4
  244.3 87.5 reduce-scatter.1
where the time goes:
time: 341 us; the launch traced here: 340 us
  waiting for transfers between devices  225 us (66%)
  matrix products  62.9 us (18%)
  local copies, waits for them, and re-layouts  27.1 us (8%)
  between operations  13.2 us (4%)
  starting transfers between devices  6.82 us (2%)
  other arithmetic  4.55 us (1%)
    reduce_scatter x1, waiting for transfers between devices, shards(): lax.psum_scatter(product.reshape((volume.shape[0] * lax.axis_size('ang'),...  87.7 us
    all_gather x1, waiting for transfers between devices, shards(): full_volume = lax.all_gather(volume, 'ang', axis=0, tiled=True)  54.7 us
    all_to_all x1, waiting for transfers between devices, shards(): lax.all_to_all(outgoing, 'pix', split_axis=0, concat_axis=0, tiled=True)  51.5 us
    all_gather x1, waiting for transfers between devices, shards(): residual = lax.all_gather(own_residual, 'pix', axis=0, tiled=True)  30.8 us
    dot_general x1, matrix products, shards(): jnp.einsum('ksq,krq->ksr', picked, projector, precision=highest)  24.8 us
    dot_general x1, matrix products, shards(): jnp.einsum('ksr,krq->ksq', back_rows, projector, precision=highest)  14.3 us
    dot_general x1, matrix products, shards(): jnp.dot(row_onehot, forward_product.reshape(tile_count, -1), precision=hi...  14.2 us
    gather x1, local copies, waits for them, and re-layouts, shards(): back_rows = jnp.take(residual, block_rows, axis=0)  11.9 us
  transfers between devices with their start and end apart: 4, of which 4 were waited for; matrix products, arithmetic and copies ran while one was open for 0% of the time, Pallas kernels for 0%

commit v1 on v0

v1 whole, which is shorter than its diff:
```python
import functools

import jax
import jax.numpy as jnp
from jax import lax
from jax.experimental import pallas as pl
from jax.experimental.pallas import tpu as pltpu
from jax.sharding import PartitionSpec as P

f32, bf16, i32 = jnp.float32, jnp.bfloat16, jnp.int32
BLANK = 4096.0
STEP = 0.5
NP, NY, NX, NC = 8, 4, 4, 2
MOST, LIVE = 4, 20
GROUP = 8
PIECES = 4
NT = (((1,), (1,)), ((), ()))
NN = (((1,), (0,)), ((), ()))
VMEM = pl.BlockSpec(memory_space=pltpu.VMEM)
SMEM = pl.BlockSpec(memory_space=pltpu.SMEM)
ANY = pl.BlockSpec(memory_space=pl.ANY)
MESH = pl.DeviceIdType.MESH


class Wires:
    def __init__(self, send, recv):
        self.send_sem, self.recv_sem, self.tags, self.started = send, recv, {}, []

    def copy(self, tag, src, dst, device):
        at = self.tags.setdefault(tag, len(self.tags))
        return pltpu.make_async_remote_copy(
            src_ref=src, dst_ref=dst, send_sem=self.send_sem.at[at], recv_sem=self.recv_sem.at[at],
            device_id=device, device_id_type=MESH,
        )

    def send(self, tag, src, dst, device):
        copy = self.copy(tag, src, dst, device)
        copy.start()
        self.started.append(copy)

    def wait(self, tag, dst, device):
        self.copy(tag, dst, dst, device).wait_recv()

    def drain(self):
        for copy in self.started:
            copy.wait_send()


def meet(devices):
    barrier = pltpu.get_barrier_semaphore()
    for device in devices:
        pl.semaphore_signal(barrier, inc=1, device_id=device, device_id_type=MESH)
    pl.semaphore_wait(barrier, len(devices))


def place():
    pix, ang = lax.axis_index("pix"), lax.axis_index("ang")
    core, x, y = lax.rem(ang, NC), lax.rem(ang // NC, NX), ang // (NC * NX)
    return pix, y, x, core


def ang_device(pix, y, x, core):
    return {"pix": pix, "ang": (y * NX + x) * NC + core}


def turn(i, by, n):
    return lax.rem(i + by + n, n)


def gather_kernel(vol, out, send, recv):
    pix, y, x, core = place()
    wires = Wires(send, recv)
    half = vol.shape[0] // 2
    quarter = half // 2
    partner = ang_device(pix, y, x, 1 - core)
    near = {
        ("x", 1): ang_device(pix, y, turn(x, 1, NX), core),
        ("x", -1): ang_device(pix, y, turn(x, -1, NX), core),
        ("y", 1): ang_device(pix, turn(y, 1, NY), x, core),
        ("y", -1): ang_device(pix, turn(y, -1, NY), x, core),
    }
    other = {"x": "y", "y": "x"}
    base = {"x": 0, "y": half}
    meet(list(near.values()) + [partner])

    def at(color, first, second, lo, n, c=core):
        dx, dy = (first, second) if color == "x" else (second, first)
        return out.at[turn(y, dy, NY), turn(x, dx, NX), c, pl.ds(base[color] + lo, n)]

    def spread(color, e, src=None):
        ref = at(color, e, 0, 0, half) if src is None else src
        for way in (1, -1):
            wires.send((color, 2, e, way), ref, at(color, e, 0, 0, half), near[other[color], way])
        wires.send((color, "p", e, 0), ref, at(color, e, 0, 0, half), partner)

    for color in ("x", "y"):
        src = vol.at[pl.ds(base[color], half)]
        for way in (1, -1):
            wires.send((color, 1, way), src, at(color, 0, 0, 0, half), near[color, way])
    for color in ("x", "y"):
        spread(color, 0, vol.at[pl.ds(base[color], half)])
    out[y, x, core] = vol[...]
    for way in (1, -1):
        for color in ("x", "y"):
            wires.wait((color, 1, way), at(color, -way, 0, 0, half), near[color, -way])
            lo = 0 if way == 1 else quarter
            part = at(color, -way, 0, lo, quarter)
            wires.send((color, 1.5, way), part, part, near[color, way])
            spread(color, -way)

    def second(e):
        for way in (1, -1):
            for color in ("x", "y"):
                ref = at(color, e, -way, 0, half)
                wires.wait((color, 2, e, way), ref, near[other[color], -way])
                lo = 0 if way == 1 else quarter
                part = at(color, e, -way, lo, quarter)
                wires.send((color, 2.5, e, way), part, part, near[other[color], way])
                wires.send((color, "p", e, -way), ref, ref, partner)

    second(0)
    for color in ("x", "y"):
        for way in (1, -1):
            lo = 0 if way == 1 else quarter
            wires.wait((color, 1.5, way), at(color, 2, 0, lo, quarter), near[color, -way])
        spread(color, 2)
    for e in (-1, 1, 2):
        second(e)
    for e in (0, -1, 1, 2):
        for color in ("x", "y"):
            for way in (1, -1):
                lo = 0 if way == 1 else quarter
                wires.wait((color, 2.5, e, way), at(color, e, 2, lo, quarter), near[other[color], -way])
            ref = at(color, e, 2, 0, half)
            wires.send((color, "p", e, 2), ref, ref, partner)
    for e in (0, -1, 1, 2):
        for f in (0, 1, -1, 2):
            for color in ("x", "y"):
                wires.wait((color, "p", e, f), at(color, e, f, 0, half, 1 - core), partner)
    wires.drain()


def gather_ang(vol):
    count = 2 * (2 + 2 + 8 + 8 + 16)
    shape = vol.shape[1:]
    return pl.pallas_call(
        gather_kernel,
        out_shape=jax.ShapeDtypeStruct((NY, NX, NC) + shape, f32),
        in_specs=[VMEM],
        out_specs=VMEM,
        scratch_shapes=[pltpu.SemaphoreType.DMA((count,)), pltpu.SemaphoreType.DMA((count,))],
        compiler_params=pltpu.CompilerParams(collective_id=0, has_side_effects=True),
        name="gather_ang",
    )(vol.reshape(shape)).reshape((NY * NX * NC,) + shape)


def scatter_kernel(grad, out, mine, far, near_in, mid, far2, near2, send, recv):
    pix, y, x, core = place()
    wires = Wires(send, recv)
    half = grad.shape[3] // 2
    quarter = half // 2
    partner = ang_device(pix, y, x, 1 - core)
    near = {
        ("x", 1): ang_device(pix, y, turn(x, 1, NX), core),
        ("x", -1): ang_device(pix, y, turn(x, -1, NX), core),
        ("y", 1): ang_device(pix, turn(y, 1, NY), x, core),
        ("y", -1): ang_device(pix, turn(y, -1, NY), x, core),
    }
    other = {"x": "y", "y": "x"}
    pos = {"x": x, "y": y}
    colors = (("x", 0, 0), ("y", 1, half))
    meet(list(near.values()) + [partner])

    def bundle(color, base, d, c):
        if color == "x":
            return grad.at[:, d, c, pl.ds(base, half)]
        return grad.at[d, :, c, pl.ds(base, half)]

    order = (2, 1, -1, 0)
    for d in order:
        for color, k, base in colors:
            at = turn(pos[color], d, 4)
            wires.send((color, "p", d), bundle(color, base, at, 1 - core), mine.at[k, at], partner)
    for d in order:
        for color, k, base in colors:
            at = turn(pos[color], d, 4)
            wires.wait((color, "p", d), mine.at[k, at], partner)
            mine[k, at] += bundle(color, base, at, core)[...]
            if d == 2:
                for w, way in enumerate((1, -1)):
                    rows = pl.ds(w * quarter, quarter)
                    wires.send((color, 1.5, way), mine.at[k, at, :, rows], far.at[k, w], near[color, way])
            elif d != 0:
                way = d
                w = 0 if way == 1 else 1
                rows = pl.ds((1 - w) * quarter, quarter)
                wires.send((color, 1, way, 0), mine.at[k, at, :, rows], near_in.at[k, w, :, rows], near[color, way])
    for w, way in enumerate((1, -1)):
        for color, k, base in colors:
            wires.wait((color, 1.5, way), far.at[k, w], near[color, -way])
            at = turn(pos[color], way, 4)
            rows = pl.ds(w * quarter, quarter)
            mine[k, at, :, rows] += far[k, w]
            wires.send((color, 1, way, 1), mine.at[k, at, :, rows], near_in.at[k, w, :, rows], near[color, way])
    for color, k, base in colors:
        at = pos[color]
        for w, way in enumerate((1, -1)):
            for part in (0, 1):
                rows = pl.ds(((1 - w) if part == 0 else w) * quarter, quarter)
                wires.wait((color, 1, way, part), near_in.at[k, w, :, rows], near[color, -way])
        mid[k] = mine[k, at] + (near_in[k, 0] + near_in[k, 1])
        second = other[color]
        at = turn(pos[second], 2, 4)
        for w, way in enumerate((1, -1)):
            rows = pl.ds(w * quarter, quarter)
            wires.send((color, 2.5, way), mid.at[k, at, rows], far2.at[k, w], near[second, way])
        for w, way in enumerate((1, -1)):
            at = turn(pos[second], way, 4)
            rows = pl.ds((1 - w) * quarter, quarter)
            wires.send((color, 2, way, 0), mid.at[k, at, rows], near2.at[k, w, rows], near[second, way])
    for w, way in enumerate((1, -1)):
        for color, k, base in colors:
            second = other[color]
            wires.wait((color, 2.5, way), far2.at[k, w], near[second, -way])
            at = turn(pos[second], way, 4)
            rows = pl.ds(w * quarter, quarter)
            mid[k, at, rows] += far2[k, w]
            wires.send((color, 2, way, 1), mid.at[k, at, rows], near2.at[k, w, rows], near[second, way])
    for color, k, base in colors:
        second = other[color]
        for w, way in enumerate((1, -1)):
            for part in (0, 1):
                rows = pl.ds(((1 - w) if part == 0 else w) * quarter, quarter)
                wires.wait((color, 2, way, part), near2.at[k, w, rows], near[second, -way])
        out[pl.ds(base, half)] = mid[k, pos[second]] + (near2[k, 0] + near2[k, 1])
    wires.drain()


def scatter_ang(grad):
    shape = grad.shape[1:]
    half, lanes = shape[0] // 2, shape[1]
    count = 2 * (4 + 2 + 4 + 2 + 4)
    return pl.pallas_call(
        scatter_kernel,
        out_shape=jax.ShapeDtypeStruct(shape, f32),
        in_specs=[VMEM],
        out_specs=VMEM,
        scratch_shapes=[
            pltpu.VMEM((2, 4, 4, half, lanes), f32),
            pltpu.VMEM((2, 2, 4, half // 2, lanes), f32),
            pltpu.VMEM((2, 2, 4, half, lanes), f32),
            pltpu.VMEM((2, 4, half, lanes), f32),
            pltpu.VMEM((2, 2, half // 2, lanes), f32),
            pltpu.VMEM((2, 2, half, lanes), f32),
            pltpu.SemaphoreType.DMA((count,)),
            pltpu.SemaphoreType.DMA((count,)),
        ],
        compiler_params=pltpu.CompilerParams(collective_id=1, has_side_effects=True),
        name="scatter_ang",
    )(grad.reshape((NY, NX, NC) + shape))


def exchange_kernel(part, weight, target, out, inbox, total, send, recv):
    me = lax.axis_index("pix")
    ang = lax.axis_index("ang")
    wires = Wires(send, recv)
    size = part.shape[1] // PIECES
    near = {way: {"pix": turn(me, way, NP), "ang": ang} for way in (1, -1)}
    meet(list(near.values()))

    def rows(i):
        return pl.ds(i * size, size)

    def goes_far(way, i):
        return (i < PIECES // 2) == (way == 1)

    order = {1: list(range(PIECES)), -1: list(range(PIECES // 2, PIECES)) + list(range(PIECES // 2))}
    pairs = [(way, order[way][n]) for n in range(PIECES) for way in (1, -1)]

    def box(way, d, i):
        return inbox.at[0 if way == 1 else 1, d - 1, rows(i)]

    def pass_on(way, d, i, src):
        wires.send(("r", way, d, i), src, box(way, d, i), near[way])

    for way, i in pairs:
        if goes_far(way, i):
            pass_on(way, 4, i, part.at[turn(me, 4, NP), rows(i)])
    for way, i in pairs:
        if not goes_far(way, i):
            pass_on(way, 3, i, part.at[turn(me, 3 * way, NP), rows(i)])
    for d in (3, 2, 1):
        for way, i in pairs:
            if d == 3 and not goes_far(way, i):
                continue
            wires.wait(("r", way, d + 1, i), box(way, d + 1, i), near[-way])
            w = 0 if way == 1 else 1
            inbox[w, d, rows(i)] += part[turn(me, d * way, NP), rows(i)]
            pass_on(way, d, i, inbox.at[w, d, rows(i)])

    def deliver(way, d, i):
        ref = out.at[turn(me, -d * way, NP), rows(i)]
        src = ref if d else total.at[rows(i)]
        wires.send(("g", way, d, i), src, ref, near[way])

    for i in range(PIECES):
        for way in (1, -1):
            wires.wait(("r", way, 1, i), box(way, 1, i), near[-way])
        summed = part[me, rows(i)] + (inbox[0, 0, rows(i)] + inbox[1, 0, rows(i)])
        residual = weight[rows(i)] * (summed - target[rows(i)])
        total[rows(i)] = residual
        for way in (1, -1):
            deliver(way, 0, i)
        out[me, rows(i)] = residual
    for d in (1, 2, 3, 4):
        for way, i in pairs:
            if d == 4 and not goes_far(way, i):
                continue
            wires.wait(("g", way, d - 1, i), out.at[turn(me, -d * way, NP), rows(i)], near[-way])
            if d < 3 or (d == 3 and goes_far(way, i)):
                deliver(way, d, i)
    wires.drain()


def exchange_pix(part, weight, target):
    count = 4 * (PIECES // 2 + 3 * PIECES)
    return pl.pallas_call(
        exchange_kernel,
        out_shape=jax.ShapeDtypeStruct(part.shape, f32),
        in_specs=[VMEM, VMEM, VMEM],
        out_specs=VMEM,
        scratch_shapes=[
            pltpu.VMEM((2, 4) + part.shape[1:], f32),
            pltpu.VMEM(part.shape[1:], f32),
            pltpu.SemaphoreType.DMA((count,)),
            pltpu.SemaphoreType.DMA((count,)),
        ],
        compiler_params=pltpu.CompilerParams(collective_id=2, has_side_effects=True),
        name="exchange_pix",
    )(part, weight, target)


def halves(value):
    high = value.astype(bf16)
    return high, (value - high.astype(f32)).astype(bf16)


def start_tiles(order, tiles, projector, held, sems):
    def one(k, _):
        pltpu.make_async_copy(projector.at[order[k]], held.at[k], sems.at[k // GROUP]).start()
        return 0

    lax.fori_loop(0, tiles, one, 0)


def wait_tiles(g, projector, held, sems):
    at = pl.ds(g * GROUP, GROUP)
    pltpu.make_async_copy(projector.at[pl.ds(0, GROUP)], held.at[at], sems.at[g]).wait()


def forward_kernel(
    first, ids, ray_counts, vol, projector, counts, part, weight, target, order, slots, cols, groups_out,
    held, sides, seen, slot_of, block_of, sems, seen_sem,
):
    n_tiles, blocks = ids.shape[0], counts.shape[0]
    width = counts.shape[1] // NP
    columns = vol.shape[0]
    fetch = pltpu.make_async_copy(counts.at[:, pl.ds(pl.multiple_of(first[0] * width, width), width)], seen, seen_sem)
    fetch.start()

    def find(b, k):
        live = lax.rem(b, MOST) < ray_counts[0, b // MOST]
        slot_of[b] = jnp.where(live, k, LIVE)
        block_of[jnp.where(live, k, LIVE)] = b
        return k + jnp.where(live, 1, 0)

    lax.fori_loop(0, blocks, find, 0, unroll=4)

    def scan(t, k):
        v = ids[t]
        slot = slot_of[v // columns]
        live = slot < LIVE
        order[k] = t
        slots[k] = slot
        cols[k] = lax.rem(v, columns)

        @pl.when(live)
        def _():
            pltpu.make_async_copy(projector.at[t], held.at[k], sems.at[k // GROUP]).start()

        return k + jnp.where(live, 1, 0)

    tiles = lax.fori_loop(0, n_tiles, scan, 0, unroll=4)
    groups = (tiles + GROUP - 1) // GROUP
    groups_out[0] = groups

    def pad(k, _):
        order[k] = 0
        slots[k] = LIVE
        cols[k] = 0
        pltpu.make_async_copy(projector.at[0], held.at[k], sems.at[k // GROUP]).start()
        return 0

    lax.fori_loop(tiles, groups * GROUP, pad, 0)

    lanes = vol.shape[2]

    def split(c, _):
        high, low = halves(vol[c])
        sides[c, :, 0:lanes] = high
        sides[c, :, lanes : 2 * lanes] = low
        sides[c, :, 2 * lanes : 3 * lanes] = high
        return 0

    lax.fori_loop(0, columns, split, 0, unroll=2)

    def clear(s, _):
        part[:, s] = jnp.zeros((NP, width, lanes), f32)
        return 0

    lax.fori_loop(0, LIVE + 1, clear, 0)
    fetch.wait()

    def weigh(s, _):
        n = seen[block_of[s]].astype(f32)
        weight[s] = n / BLANK
        target[s] = jnp.log(BLANK / n)
        return 0

    lax.fori_loop(0, LIVE, weigh, 0)

    def group(g, _):
        wait_tiles(g, projector, held, sems)
        products = []
        for u in range(GROUP):
            k = g * GROUP + u
            high, low = halves(held[k])
            products.append(
                lax.dot_general(
                    sides[cols[k]], jnp.concatenate([high, high, low], axis=1), NT, preferred_element_type=f32
                )
            )
        for u in range(GROUP):
            part[:, slots[g * GROUP + u]] += products[u].reshape(NP, width, lanes)
        return 0

    lax.fori_loop(0, groups, group, 0)


def forward(ids, ray_counts, vol, projector, counts):
    n_tiles, rays, lanes = projector.shape
    blocks, slices, _ = counts.shape
    width = slices // NP
    n_groups = -(-n_tiles // GROUP)
    padded = n_groups * GROUP
    first = lax.axis_index("pix").astype(i32).reshape(1)
    shape = jax.ShapeDtypeStruct
    return pl.pallas_call(
        forward_kernel,
        out_shape=(
            shape((NP, LIVE + 1, width, rays), f32),
            shape((LIVE, width, rays), f32),
            shape((LIVE, width, rays), f32),
            shape((padded,), i32),
            shape((padded,), i32),
            shape((padded,), i32),
            shape((1,), i32),
        ),
        in_specs=[SMEM, SMEM, SMEM, VMEM, ANY, ANY],
        out_specs=(VMEM, VMEM, VMEM, SMEM, SMEM, SMEM, SMEM),
        scratch_shapes=[
            pltpu.VMEM((padded, rays, lanes), f32),
            pltpu.VMEM((vol.shape[0], slices, 3 * lanes), bf16),
            pltpu.VMEM((blocks, width, rays), i32),
            pltpu.SMEM((blocks,), i32),
            pltpu.SMEM((LIVE + 1,), i32),
            pltpu.SemaphoreType.DMA((n_groups,)),
            pltpu.SemaphoreType.DMA(()),
        ],
        compiler_params=pltpu.CompilerParams(vmem_limit_bytes=56 << 20),
        name="forward",
    )(first, ids, ray_counts, vol, projector, counts)


def backward_kernel(order, slots, cols, groups_in, residual, projector, grad, held, sides, sems):
    groups = groups_in[0]
    start_tiles(order, groups * GROUP, projector, held, sems)
    live, slices, lanes = sides.shape[0] - 1, sides.shape[1], grad.shape[2]

    def split(s, _):
        high, low = halves(residual[:, s].reshape(slices, lanes))
        sides[s, :, 0:lanes] = high
        sides[s, :, lanes : 2 * lanes] = low
        sides[s, :, 2 * lanes : 3 * lanes] = high
        return 0

    lax.fori_loop(0, live, split, 0, unroll=2)
    sides[live] = jnp.zeros(sides.shape[1:], bf16)

    def clear(c, _):
        grad[c] = jnp.zeros(grad.shape[1:], f32)
        return 0

    lax.fori_loop(0, grad.shape[0], clear, 0)

    def group(g, _):
        wait_tiles(g, projector, held, sems)
        products = []
        for u in range(GROUP):
            k = g * GROUP + u
            high, low = halves(held[k])
            products.append(
                lax.dot_general(
                    sides[slots[k]], jnp.concatenate([high, high, low], axis=0), NN, preferred_element_type=f32
                )
            )
        for u in range(GROUP):
            grad[cols[g * GROUP + u]] += products[u]
        return 0

    lax.fori_loop(0, groups, group, 0)


def backward(order, slots, cols, groups, residual, projector, columns):
    n_tiles, rays, lanes = projector.shape
    padded = order.shape[0]
    slices = residual.shape[0] * residual.shape[2]
    return pl.pallas_call(
        backward_kernel,
        out_shape=jax.ShapeDtypeStruct((columns, slices, lanes), f32),
        in_specs=[SMEM, SMEM, SMEM, SMEM, VMEM, ANY],
        out_specs=VMEM,
        scratch_shapes=[
            pltpu.VMEM((padded, rays, lanes), f32),
            pltpu.VMEM((LIVE + 1, slices, 3 * rays), bf16),
            pltpu.SemaphoreType.DMA((padded // GROUP,)),
        ],
        compiler_params=pltpu.CompilerParams(vmem_limit_bytes=56 << 20),
        name="backward",
    )(order, slots, cols, groups, residual, projector)


def shards(volume, projector, tile_ids, counts, ray_counts):
    full = gather_ang(volume)
    part, weight, target, order, slots, cols, groups = forward(tile_ids, ray_counts, full, projector, counts)
    residual = exchange_pix(part, weight, target)
    terms = backward(order, slots, cols, groups, residual, projector, full.shape[0])
    gradient = scatter_ang(terms)
    return volume - STEP * gradient


def solution(mesh):
    placed = (
        P(("pix", "ang"), None, None),
        P(("pix", "ang"), None, None),
        P(("pix", "ang")),
        P("ang", None, None),
        P("ang", None),
    )
    return jax.shard_map(
        shards, mesh=mesh, in_specs=placed, out_specs=P(("pix", "ang"), None, None), check_vma=False
    )
```

time: 341 us -> 108 us (0.32)
  waiting for transfers between devices: 225 us -> 0 us
  Pallas kernels: 0 us -> 107 us
  matrix products: 62.9 us -> 0 us
  local copies, waits for them, and re-layouts: 27.1 us -> 0.01 us
  between operations: 13.2 us -> 0.06 us
  starting transfers between devices: 6.82 us -> 0 us
    pallas_call x0 -> x5, Pallas kernels: none -> 107 us  [the longest x1 36.8 us: exchange_pix(): pl.pallas_call(exchange_kernel, out_shape=jax.ShapeDtypeStruct(part.shape...]
    reduce_scatter x1 -> x0, waiting for transfers between devices: 87.7 us -> none  [shards(): lax.psum_scatter(product.reshape((volume.shape[0] * lax.axis_size('ang'),...]
    all_gather x2 -> x0, waiting for transfers between devices: 85.5 us -> none  [the longest x1 54.7 us: shards(): full_volume = lax.all_gather(volume, 'ang', axis=0, tiled=True)]
    dot_general x4 -> x0, matrix products: 62.9 us -> none  [the longest x1 24.8 us: shards(): jnp.einsum('ksq,krq->ksr', picked, projector, precision=highest)]
    all_to_all x1 -> x0, waiting for transfers between devices: 51.5 us -> none  [shards(): lax.all_to_all(outgoing, 'pix', split_axis=0, concat_axis=0, tiled=True)]
    gather x2 -> x0, local copies, waits for them, and re-layouts: 23.7 us -> none  [the longest x1 11.9 us: shards(): back_rows = jnp.take(residual, block_rows, axis=0)]
    all_to_all x1 -> x0, starting transfers between devices: 6.73 us -> none  [shards(): lax.all_to_all(outgoing, 'pix', split_axis=0, concat_axis=0, tiled=True)]
  transfers between devices with their start and end apart: 4 -> 0, of which waited for: 4 -> 0; matrix products, arithmetic and copies ran while one was open for 0% -> 0% of each run, Pallas kernels for 0% -> 0%
where the time goes in v1:
time: 108 us
  Pallas kernels  107 us (99%)
  other arithmetic  1.48 us (1%)
    pallas_call x1, Pallas kernels, exchange_pix(): pl.pallas_call(exchange_kernel, out_shape=jax.ShapeDtypeStruct(part.shape...  36.8 us
    pallas_call x1, Pallas kernels, scatter_ang(): pl.pallas_call(scatter_kernel, out_shape=jax.ShapeDtypeStruct(shape, f32)...  24.9 us
    pallas_call x1, Pallas kernels, gather_ang(): pl.pallas_call(gather_kernel, out_shape=jax.ShapeDtypeStruct((NY, NX, NC)...  23.2 us
    pallas_call x1, Pallas kernels, forward(): pl.pallas_call(forward_kernel, out_shape=(shape((NP, LIVE + 1, width, ray...  12.3 us
    pallas_call x1, Pallas kernels, backward(): pl.pallas_call(backward_kernel, out_shape=jax.ShapeDtypeStruct((columns,...  9.49 us

profile of v1, /device:TPU:1, one launch (start us, length us, event | category | flops | bytes accessed | tf_op | source)
XLA Modules:
  0.0 108.2 jit_solution(1524305009250855505)
XLA Ops:
  0.0 23.2 %gather_ang.1 = f32[4,4,2,128,128]{4,3,2,1,0:T(8,128)} custom-call(f32[128,128]{1,0:T(8,128)} %bitcast.8), custom_call_target="tpu_custom_call" | custom-call | tf_op jit(solution)/shard_map/gather_ang/pallas_call | solution.py:146
  23.2 12.3 %forward.1 = (f32[8,21,16,128]{3,2,1,0:T(8,128)}, f32[20,16,128]{2,1,0:T(8,128)}, f32[20,16,128]{2,1,0:T(8,128)}, s32[160]{0:T(256)}, s32[160]{0:T(256)}, /*index=5*/s32[160]{0:T(256)}, s32[1]{0:T(128)}) custom-call(s32[1]{0:T(128)} %bitcast.first, s32[160]{0:T(256)} %ids.1, s32[1,8]{1,0:T(1,128)} %ray_counts.1, f32[32,128,128]{2,1,0:T(8,128)} %bitcast.7, ...), custom_call_target="tpu_custom_call" | custom-call | tf_op jit(solution)/shard_map/forward/pallas_call | solution.py:458
  35.5 36.8 %exchange_pix.1.residual = f32[8,21,16,128]{3,2,1,0:T(8,128)} custom-call(f32[8,21,16,128]{3,2,1,0:T(8,128)} %get-tuple-element.16.part, f32[20,16,128]{2,1,0:T(8,128)} %get-tuple-element.17.weight, f32[20,16,128]{2,1,0:T(8,128)} %get-tuple-element.18.target), custom_call_target="tpu_custom_call" | custom-call | tf_op jit(solution)/shard_map/exchange_pix/pallas_call | solution.py:327
  72.3 9.5 %backward.1 = f32[32,128,128]{2,1,0:T(8,128)} custom-call(s32[160]{0:T(256)} %get-tuple-element.12.order, s32[160]{0:T(256)} %get-tuple-element.13.slots, s32[160]{0:T(256)} %get-tuple-element.14.cols, s32[1]{0:T(128)} %get-tuple-element.15.groups_in, f32[8,21,16,128]{3,2,1,0:T(8,128)} %exchange_pix.1.residual, f32[160,128,128]{2,1,0:T(8,128)} %projector.3), custom_call_target="tpu_custom_call" | custom-call | tf_op jit(solution)/shard_map/backward/pallas_call | solution.py:528
  81.8 0.0 copy-start
  81.8 24.9 %scatter_ang.1 = f32[128,128]{1,0:T(8,128)} custom-call(f32[4,4,2,128,128]{4,3,2,1,0:T(8,128)} %bitcast.6), custom_call_target="tpu_custom_call" | custom-call | tf_op jit(solution)/shard_map/scatter_ang/pallas_call | solution.py:243
  106.7 0.0 copy-done
  106.7 1.5 %bitcast_subtract_fusion = f32[1,128,128]{2,1,0:T(8,128)} fusion(f32[1,128,128]{2,1,0:T(8,128)S(1)} %copy-done, f32[128,128]{1,0:T(8,128)} %scatter_ang.1), kind=kLoop, calls=%fused_computation | loop fusion | flops 32768 | bytes 196608 | tf_op jit(solution)/shard_map/sub | solution.py:549
Async XLA Ops:
  81.8 24.9 %copy-start = (f32[1,128,128]{2,1,0:T(8,128)S(1)}, f32[1,128,128]{2,1,0:T(8,128)}, u32[]{:S(2)}) copy-start(f32[1,128,128]{2,1,0:T(8,128)} %param.5) | copy-start | bytes 196612

commit v2 on v0

v2 whole, which is shorter than its diff:
```python
import functools

import jax
import jax.numpy as jnp
from jax import lax
from jax.experimental import pallas as pl
from jax.experimental.pallas import tpu as pltpu
from jax.sharding import PartitionSpec as P

f32, bf16, i32 = jnp.float32, jnp.bfloat16, jnp.int32
BLANK = 4096.0
STEP = 0.5
NP, NY, NX, NC = 8, 4, 4, 2
COLS = NY * NX * NC
MOST, LIVE = 4, 20
WIDTH = 16
HALF = 64
PIECES = 4
BATCH = 16
BUFFERS = 3
UNROLL = 8
LANES = 256
NN = (((1,), (0,)), ((), ()))
VMEM = pl.BlockSpec(memory_space=pltpu.VMEM)
SMEM = pl.BlockSpec(memory_space=pltpu.SMEM)
ANY = pl.BlockSpec(memory_space=pl.ANY)
MESH = pl.DeviceIdType.MESH
OFFSETS = sorted(
    ((dy, dx) for dy in range(NY) for dx in range(NX) if (dy, dx) != (0, 0)),
    key=lambda o: -(min(o[0], NY - o[0]) + min(o[1], NX - o[1])),
)


class Wires:
    def __init__(self, send, recv):
        self.send_sem, self.recv_sem, self.tags, self.started = send, recv, {}, []

    def copy(self, tag, src, dst, device):
        at = self.tags.setdefault(tag, len(self.tags))
        return pltpu.make_async_remote_copy(
            src_ref=src, dst_ref=dst, send_sem=self.send_sem.at[at], recv_sem=self.recv_sem.at[at],
            device_id=device, device_id_type=MESH,
        )

    def send(self, tag, src, dst, device):
        copy = self.copy(tag, src, dst, device)
        copy.start()
        self.started.append(copy)

    def wait(self, tag, dst, device):
        self.copy(tag, dst, dst, device).wait_recv()

    def drain(self):
        for copy in self.started:
            copy.wait_send()


def meet(devices):
    barrier = pltpu.get_barrier_semaphore()
    for device in devices:
        pl.semaphore_signal(barrier, inc=1, device_id=device, device_id_type=MESH)
    pl.semaphore_wait(barrier, len(devices))


def turn(i, by, n):
    return lax.rem(i + by + n, n)


def rel(d):
    return (d - 2) % NP


def halves(value):
    high = value.astype(bf16)
    return high, (value - high.astype(f32)).astype(bf16)


def dot(a, b):
    return lax.dot_general(a, b, NN, preferred_element_type=f32)


def turned(row):
    return jnp.transpose(jnp.broadcast_to(row, (LANES, LANES)))


def down(value):
    return jnp.sum(value, axis=0, keepdims=True, dtype=i32)


def tabulate(ids, ray_counts, work, table):
    n = ids.shape[1]
    work[...] = jnp.zeros(work.shape, i32)
    work[0:1, 0:n] = ids[...]
    v = work[0:1]
    lane = lax.broadcasted_iota(i32, (1, LANES), 1)
    lanes = lax.broadcasted_iota(i32, (LANES, LANES), 1)

    def slots_of(block):
        owner, j = block >> 2, block & (MOST - 1)
        held = jnp.zeros_like(block)
        before = jnp.zeros_like(block)
        running = jnp.int32(0)
        for o in range(NP):
            here = ray_counts[0, o]
            held = jnp.where(owner == o, here, held)
            before = jnp.where(owner == o, running, before)
            running = running + here
        return j < held, before + j

    live, slot = slots_of(v >> 5)
    live = live & (lane < n)
    col = v & (COLS - 1)
    slot = jnp.where(live, slot, 31)
    payload = turned(lane * 1024 + slot * 32 + col)
    for at, key, name in ((0, slot * 32 + col, slot), (1, col * 32 + slot, jnp.where(live, col, 63))):
        key = jnp.where(live, key, 2048 + lane)
        rank = down(jnp.where(turned(key) < key, 1, 0))
        table[at : at + 1] = down(jnp.where(turned(rank) == lanes, payload, 0))
        names = turned(name)
        count = down(jnp.where(names == lanes, 1, 0))
        upto = down(jnp.where(names <= lanes, 1, 0))
        table[at + 2 : at + 3] = jnp.where(count > 0, upto, 0)
    live, slot = slots_of(jnp.minimum(lane, NP * MOST - 1))
    names = turned(jnp.where(live & (lane < NP * MOST), slot, 63))
    which = lax.broadcasted_iota(i32, (LANES, LANES), 0)
    table[4:5] = down(jnp.where(names == lanes, which, 0))


def within(value, bound):
    return jnp.minimum(jnp.maximum(value, 0), bound - 1)


def step_kernel(
    ids, ray_counts, vol, projector, counts, out,
    rotated, full, stage, tiles, flipped, sides, back, sums, part, inbox, weight, target, residual, total, seen,
    grad, mine, terms, work, table, lists, tile_sems, other_sems, send, recv,
):
    me, ang = lax.axis_index("pix"), lax.axis_index("ang")
    core, x, y = lax.rem(ang, NC), lax.rem(ang // NC, NX), ang // (NC * NX)
    wires = Wires(send, recv)
    n_tiles = projector.shape[0]
    batches = n_tiles // BATCH

    def peer(dy, dx, c=core):
        return {"pix": me, "ang": (turn(y, dy, NY) * NX + turn(x, dx, NX)) * NC + c}

    partner = peer(0, 0, 1 - core)
    near = {way: {"pix": turn(me, way, NP), "ang": ang} for way in (1, -1)}

    def slices_of(i):
        return pl.ds(pl.multiple_of(turn(me, 2 + i, NP) * WIDTH, WIDTH), WIDTH)

    def chunk(k):
        return pl.ds(k * HALF, HALF)

    def fetch(b):
        return pltpu.make_async_copy(
            projector.at[pl.ds(b * BATCH, BATCH)], stage.at[b % BUFFERS], tile_sems.at[b]
        )

    look = pltpu.make_async_copy(counts.at[:, slices_of(rel(0))], seen, other_sems.at[0])
    for b in range(BUFFERS):
        fetch(b).start()
    look.start()
    for i in range(NP):
        rotated[i * WIDTH : (i + 1) * WIDTH] = vol[0, slices_of(i)]
    meet([peer(dy, dx) for dy, dx in OFFSETS] + [partner, near[1], near[-1]])

    for k in range(2):
        for dy, dx in OFFSETS:
            wires.send(("v", k, dy, dx), rotated.at[chunk(k)], full.at[y, x, core, chunk(k)], peer(dy, dx))
        wires.send(("p", k, 0, 0), rotated.at[chunk(k)], full.at[y, x, core, chunk(k)], partner)

    tabulate(ids, ray_counts, work, table)
    give = pltpu.make_async_copy(table, lists, other_sems.at[1])
    give.start()

    def prepare(b):
        fetch(b).wait()

        def one(t, _):
            value = stage[b % BUFFERS, t]
            high, low = halves(value)
            tiles[b * BATCH + t, 0] = high
            tiles[b * BATCH + t, 1] = low
            high, low = halves(jnp.transpose(value))
            flipped[b * BATCH + t, 0] = high
            flipped[b * BATCH + t, 1] = low
            return 0

        lax.fori_loop(0, BATCH, one, 0, unroll=2)
        if b + BUFFERS < batches:
            fetch(b + BUFFERS).start()

    def split_volume(k, yy, xx, c):
        high, low = halves(full[yy, xx, c, chunk(k)])
        at = (yy * NX + xx) * NC + c
        sides[k, at, 0:HALF] = high
        sides[k, at, HALF : 2 * HALF] = low

    def receive_volume(k):
        for dy, dx in OFFSETS:
            ref = full.at[turn(y, -dy, NY), turn(x, -dx, NX), core, chunk(k)]
            wires.wait(("v", k, dy, dx), ref, peer(-dy, -dx))
            wires.send(("p", k, dy, dx), ref, ref, partner)
            split_volume(k, turn(y, -dy, NY), turn(x, -dx, NX), core)

    def receive_partner(k):
        for dy, dx in [(0, 0)] + OFFSETS:
            ref = full.at[turn(y, -dy, NY), turn(x, -dx, NX), 1 - core, chunk(k)]
            wires.wait(("p", k, dy, dx), ref, partner)
            split_volume(k, turn(y, -dy, NY), turn(x, -dx, NX), 1 - core)

    def products(row, shift, left, k, right, first, count):
        def some(g, _):
            at = first + g * UNROLL
            running = sums[at]
            before = lists[row, jnp.maximum(at - 1, 0)]
            for u in range(UNROLL):
                entry = lists[row, at + u]
                name = (entry >> shift) & 31
                same = jnp.where(name == ((before >> shift) & 31), 1.0, 0.0)
                operand = (entry >> (5 - shift)) & 31
                t = within(entry >> 10, n_tiles)
                both = dot(left[k, operand], right[t, 0])
                value = both[0:HALF] + both[HALF : 2 * HALF] + dot(left[k, operand, 0:HALF], right[t, 1])
                running = value + running * same
                sums[at + u + 1] = running
                before = entry
            return 0

        lax.fori_loop(0, count // UNROLL, some, 0)

    def forward(k, first, count):
        products(0, 5, sides, k, flipped, first, count)

    def backward(k, first, count):
        products(1, 0, back, k, tiles, first, count)

    def take_part(k):
        def one(j, _):
            value = sums[within(lists[2, j], n_tiles + 1)]
            for i in range(4):
                part[4 * k + i, j] = value[i * WIDTH : (i + 1) * WIDTH]
            return 0

        lax.fori_loop(0, LIVE, one, 0, unroll=2)

    def weigh():
        look.wait()

        def one(j, _):
            n = seen[within(lists[4, j], NP * MOST)].astype(f32)
            weight[j] = n / BLANK
            target[j] = jnp.log(BLANK / n)
            return 0

        lax.fori_loop(0, LIVE, one, 0)

    size = LIVE // PIECES
    order = {1: list(range(PIECES)), -1: list(range(PIECES // 2, PIECES)) + list(range(PIECES // 2))}
    pairs = [(way, order[way][n]) for n in range(PIECES) for way in (1, -1)]

    def rows(i):
        return pl.ds(i * size, size)

    def goes_far(way, i):
        return (i < PIECES // 2) == (way == 1)

    def box(way, d, i):
        return inbox.at[0 if way == 1 else 1, d - 1, rows(i)]

    def pass_on(way, d, i, src):
        wires.send(("r", way, d, i), src, box(way, d, i), near[way])

    def start_sums():
        for way, i in pairs:
            if goes_far(way, i):
                pass_on(way, 4, i, part.at[rel(4), rows(i)])
        for way, i in pairs:
            if not goes_far(way, i):
                pass_on(way, 3, i, part.at[rel(3 * way), rows(i)])

    def relay_sums(d):
        for way, i in pairs:
            if d == 3 and not goes_far(way, i):
                continue
            wires.wait(("r", way, d + 1, i), box(way, d + 1, i), near[-way])
            w = 0 if way == 1 else 1
            inbox[w, d, rows(i)] += part[rel(d * way), rows(i)]
            pass_on(way, d, i, inbox.at[w, d, rows(i)])

    def deliver(way, d, i):
        ref = residual.at[rel(-d * way), rows(i)]
        there = residual.at[rel(-(d + 1) * way), rows(i)]
        src = ref if d else total.at[rows(i)]
        wires.send(("g", way, d, i), src, there, near[way])

    def finish_sums():
        for i in [pairs[2 * n][1] for n in range(PIECES)]:
            for way in (1, -1):
                wires.wait(("r", way, 1, i), box(way, 1, i), near[-way])
            summed = part[rel(0), rows(i)] + (inbox[0, 0, rows(i)] + inbox[1, 0, rows(i)])
            value = weight[rows(i)] * (summed - target[rows(i)])
            total[rows(i)] = value
            for way in (1, -1):
                deliver(way, 0, i)
            residual[rel(0), rows(i)] = value

    def relay_residual(d):
        for way, i in pairs:
            if d == 4 and not goes_far(way, i):
                continue
            wires.wait(("g", way, d - 1, i), residual.at[rel(-d * way), rows(i)], near[-way])
            if d < 3 or (d == 3 and goes_far(way, i)):
                deliver(way, d, i)

    def split_residual(k):
        def one(j, _):
            for i in range(4):
                high, low = halves(residual[4 * k + i, j])
                back[k, j, i * WIDTH : (i + 1) * WIDTH] = high
                back[k, j, HALF + i * WIDTH : HALF + (i + 1) * WIDTH] = low
            return 0

        lax.fori_loop(0, LIVE, one, 0, unroll=2)

    def start_grad(k):
        for c in range(COLS):
            grad[k, c // (NX * NC), (c // NC) % NX, c % NC] = sums[within(lists[3, c], n_tiles + 1)]
        wires.send(("q", k), grad.at[k, :, :, 1 - core], mine.at[k], partner)

    def spread_grad(k):
        wires.wait(("q", k), mine.at[k], partner)
        for n, (dy, dx) in enumerate(OFFSETS):
            yy, xx = turn(y, dy, NY), turn(x, dx, NX)
            mine[k, yy, xx] += grad[k, yy, xx, core]
            wires.send(("t", k, dy, dx), mine.at[k, yy, xx], terms.at[k, n], peer(dy, dx))

    def finish_grad(k):
        value = mine[k, y, x] + grad[k, y, x, core]
        for n, (dy, dx) in enumerate(OFFSETS):
            wires.wait(("t", k, dy, dx), terms.at[k, n], peer(-dy, -dx))
            value = value + terms[k, n]
        for i in range(4):
            out[0, slices_of(4 * k + i)] = value[i * WIDTH : (i + 1) * WIDTH]

    full[y, x, core] = rotated[...]
    for k in range(2):
        split_volume(k, y, x, core)
    sums[0] = jnp.zeros(sums.shape[1:], f32)
    for j in range(LIVE, 32):
        back[0, j] = jnp.zeros(back.shape[2:], bf16)
        back[1, j] = jnp.zeros(back.shape[2:], bf16)
    for b in range(batches - 3):
        prepare(b)
    receive_volume(0)
    for b in range(batches - 3, batches):
        prepare(b)
    give.wait()
    receive_partner(0)
    quarter = n_tiles // 4
    forward(0, 0, n_tiles)
    take_part(0)
    start_sums()
    receive_volume(1)
    receive_partner(1)
    forward(1, 0, 2 * quarter)
    weigh()
    relay_sums(3)
    forward(1, 2 * quarter, 2 * quarter)
    take_part(1)
    relay_sums(2)
    relay_sums(1)
    finish_sums()
    relay_residual(1)
    relay_residual(2)
    split_residual(1)
    backward(1, 0, 2 * quarter)
    relay_residual(3)
    backward(1, 2 * quarter, 2 * quarter)
    start_grad(1)
    relay_residual(4)
    split_residual(0)
    backward(0, 0, quarter)
    spread_grad(1)
    backward(0, quarter, 3 * quarter)
    start_grad(0)
    finish_grad(1)
    spread_grad(0)
    finish_grad(0)
    wires.drain()


def shards(volume, projector, tile_ids, counts, ray_counts):
    n_tiles, rays, lanes = projector.shape
    slices = volume.shape[1]
    n_sems = 2 * (2 * len(OFFSETS) + 1) + 4 * (PIECES // 2 + 3 * PIECES) + 2 * (len(OFFSETS) + 1)
    gradient = pl.pallas_call(
        step_kernel,
        out_shape=jax.ShapeDtypeStruct(volume.shape, f32),
        in_specs=[VMEM, SMEM, VMEM, ANY, ANY],
        out_specs=VMEM,
        scratch_shapes=[
            pltpu.VMEM((slices, lanes), f32),
            pltpu.VMEM((NY, NX, NC, slices, lanes), f32),
            pltpu.VMEM((BUFFERS, BATCH, rays, lanes), f32),
            pltpu.VMEM((n_tiles, 2, rays, lanes), bf16),
            pltpu.VMEM((n_tiles, 2, lanes, rays), bf16),
            pltpu.VMEM((2, COLS, 2 * HALF, lanes), bf16),
            pltpu.VMEM((2, 32, 2 * HALF, rays), bf16),
            pltpu.VMEM((n_tiles + 1, HALF, lanes), f32),
            pltpu.VMEM((NP, LIVE, WIDTH, rays), f32),
            pltpu.VMEM((2, 4, LIVE, WIDTH, rays), f32),
            pltpu.VMEM((LIVE, WIDTH, rays), f32),
            pltpu.VMEM((LIVE, WIDTH, rays), f32),
            pltpu.VMEM((NP, LIVE, WIDTH, rays), f32),
            pltpu.VMEM((LIVE, WIDTH, rays), f32),
            pltpu.VMEM((counts.shape[0], WIDTH, rays), i32),
            pltpu.VMEM((2, NY, NX, NC, HALF, lanes), f32),
            pltpu.VMEM((2, NY, NX, HALF, lanes), f32),
            pltpu.VMEM((2, len(OFFSETS), HALF, lanes), f32),
            pltpu.VMEM((8, LANES), i32),
            pltpu.VMEM((8, LANES), i32),
            pltpu.SMEM((8, LANES), i32),
            pltpu.SemaphoreType.DMA((n_tiles // BATCH,)),
            pltpu.SemaphoreType.DMA((2,)),
            pltpu.SemaphoreType.DMA((n_sems,)),
            pltpu.SemaphoreType.DMA((n_sems,)),
        ],
        compiler_params=pltpu.CompilerParams(
            collective_id=0, has_side_effects=True, vmem_limit_bytes=62 << 20
        ),
        name="step",
    )(tile_ids.reshape(1, n_tiles), ray_counts, volume, projector, counts)
    return volume - STEP * gradient


def solution(mesh):
    placed = (
        P(("pix", "ang"), None, None),
        P(("pix", "ang"), None, None),
        P(("pix", "ang")),
        P("ang", None, None),
        P("ang", None),
    )
    return jax.shard_map(
        shards, mesh=mesh, in_specs=placed, out_specs=P(("pix", "ang"), None, None), check_vma=False
    )
```

time: 341 us -> 85.9 us (0.25)
  waiting for transfers between devices: 225 us -> 0 us
  Pallas kernels: 0 us -> 84.1 us
  matrix products: 62.9 us -> 0 us
  local copies, waits for them, and re-layouts: 27.1 us -> 0.01 us
  between operations: 13.2 us -> 0.02 us
  starting transfers between devices: 6.82 us -> 0 us
    reduce_scatter x1 -> x0, waiting for transfers between devices: 87.7 us -> none  [shards(): lax.psum_scatter(product.reshape((volume.shape[0] * lax.axis_size('ang'),...]
    all_gather x2 -> x0, waiting for transfers between devices: 85.5 us -> none  [the longest x1 54.7 us: shards(): full_volume = lax.all_gather(volume, 'ang', axis=0, tiled=True)]
    pallas_call x0 -> x1, Pallas kernels: none -> 84.1 us  [shards(): pl.pallas_call(step_kernel, out_shape=jax.ShapeDtypeStruct(volume.shape,...]
    dot_general x4 -> x0, matrix products: 62.9 us -> none  [the longest x1 24.8 us: shards(): jnp.einsum('ksq,krq->ksr', picked, projector, precision=highest)]
    all_to_all x1 -> x0, waiting for transfers between devices: 51.5 us -> none  [shards(): lax.all_to_all(outgoing, 'pix', split_axis=0, concat_axis=0, tiled=True)]
    gather x2 -> x0, local copies, waits for them, and re-layouts: 23.7 us -> none  [the longest x1 11.9 us: shards(): back_rows = jnp.take(residual, block_rows, axis=0)]
    all_to_all x1 -> x0, starting transfers between devices: 6.73 us -> none  [shards(): lax.all_to_all(outgoing, 'pix', split_axis=0, concat_axis=0, tiled=True)]
  transfers between devices with their start and end apart: 4 -> 0, of which waited for: 4 -> 0; matrix products, arithmetic and copies ran while one was open for 0% -> 0% of each run, Pallas kernels for 0% -> 0%
where the time goes in v2:
time: 85.9 us; the launch traced here: 85.6 us
  Pallas kernels  84.1 us (98%)
  other arithmetic  1.48 us (2%)
    pallas_call x1, Pallas kernels, shards(): pl.pallas_call(step_kernel, out_shape=jax.ShapeDtypeStruct(volume.shape,...  84.1 us

profile of v2, /device:TPU:1, one launch (start us, length us, event | category | flops | bytes accessed | tf_op | source)
XLA Modules:
  0.0 85.6 jit_solution(10992539075129818744)
XLA Ops:
  0.0 0.0 copy-start
  0.0 84.1 %step.1 = f32[1,128,128]{2,1,0:T(8,128)} custom-call(s32[1,160]{1,0:T(1,128)} %bitcast.1, s32[1,8]{1,0:T(1,128)} %ray_counts.1, f32[1,128,128]{2,1,0:T(8,128)} %vol.1, f32[160,128,128]{2,1,0:T(8,128)} %projector.1, s32[32,128,128]{2,1,0:T(8,128)} %counts.1), custom_call_target="tpu_custom_call" | custom-call | tf_op jit(solution)/shard_map/step/pallas_call | solution.py:399
  84.1 0.0 copy-done
  84.1 1.5 %multiply_subtract_fusion = f32[1,128,128]{2,1,0:T(8,128)} fusion(f32[1,128,128]{2,1,0:T(8,128)S(1)} %copy-done, f32[1,128,128]{2,1,0:T(8,128)} %step.1), kind=kLoop, calls=%fused_computation | loop fusion | flops 32768 | bytes 196608 | tf_op jit(solution)/shard_map/sub | solution.py:436
Async XLA Ops:
  0.0 84.1 %copy-start = (f32[1,128,128]{2,1,0:T(8,128)S(1)}, f32[1,128,128]{2,1,0:T(8,128)}, u32[]{:S(2)}) copy-start(f32[1,128,128]{2,1,0:T(8,128)} %vol.1) | copy-start | bytes 196612

commit v3 on v2

--- a/solution.py
+++ b/solution.py
@@ -14,11 +14,12 @@
 COLS = NY * NX * NC
 MOST, LIVE = 4, 20
 WIDTH = 16
-HALF = 64
+PLACES = (3, 4, -3, 2, -2, -1, 0, 1)
+CHUNKS = ((0, 3), (3, 2), (5, 3))
 PIECES = 4
 BATCH = 16
 BUFFERS = 3
-UNROLL = 8
+UNROLL = 40
 LANES = 256
 NN = (((1,), (0,)), ((), ()))
 VMEM = pl.BlockSpec(memory_space=pltpu.VMEM)
@@ -29,6 +30,7 @@
     ((dy, dx) for dy in range(NY) for dx in range(NX) if (dy, dx) != (0, 0)),
     key=lambda o: -(min(o[0], NY - o[0]) + min(o[1], NX - o[1])),
 )
+BY_ROW = [(dy, dx) for dy in (2, 1, 3, 0) for dx in (2, 1, 3, 0) if (dy, dx) != (0, 0)]
 
 
 class Wires:
@@ -55,11 +57,10 @@
             copy.wait_send()
 
 
-def meet(devices):
+def greet(devices):
     barrier = pltpu.get_barrier_semaphore()
     for device in devices:
         pl.semaphore_signal(barrier, inc=1, device_id=device, device_id_type=MESH)
-    pl.semaphore_wait(barrier, len(devices))
 
 
 def turn(i, by, n):
@@ -67,7 +68,7 @@
 
 
 def rel(d):
-    return (d - 2) % NP
+    return [p % NP for p in PLACES].index(d % NP)
 
 
 def halves(value):
@@ -132,12 +133,13 @@
 
 def step_kernel(
     ids, ray_counts, vol, projector, counts, out,
-    rotated, full, stage, tiles, flipped, sides, back, sums, part, inbox, weight, target, residual, total, seen,
-    grad, mine, terms, work, table, lists, tile_sems, other_sems, send, recv,
+    rotated, full, stage, tiles, flipped, side0, side1, side2, back0, back1, back2, sums, part, inbox, weight, target,
+    residual, total, seen, grad, mine, terms, work, table, lists, tile_sems, other_sems, send, recv,
 ):
     me, ang = lax.axis_index("pix"), lax.axis_index("ang")
     core, x, y = lax.rem(ang, NC), lax.rem(ang // NC, NX), ang // (NC * NX)
     wires = Wires(send, recv)
+    sides, back = (side0, side1, side2), (back0, back1, back2)
     n_tiles = projector.shape[0]
     batches = n_tiles // BATCH
 
@@ -146,12 +148,17 @@
 
     partner = peer(0, 0, 1 - core)
     near = {way: {"pix": turn(me, way, NP), "ang": ang} for way in (1, -1)}
+    friends = [peer(dy, dx) for dy, dx in OFFSETS] + [partner, near[1], near[-1]]
+    greet(friends)
 
     def slices_of(i):
-        return pl.ds(pl.multiple_of(turn(me, 2 + i, NP) * WIDTH, WIDTH), WIDTH)
+        return pl.ds(pl.multiple_of(turn(me, PLACES[i], NP) * WIDTH, WIDTH), WIDTH)
+
+    def length(k):
+        return CHUNKS[k][1] * WIDTH
 
     def chunk(k):
-        return pl.ds(k * HALF, HALF)
+        return pl.ds(CHUNKS[k][0] * WIDTH, length(k))
 
     def fetch(b):
         return pltpu.make_async_copy(
@@ -164,9 +171,9 @@
     look.start()
     for i in range(NP):
         rotated[i * WIDTH : (i + 1) * WIDTH] = vol[0, slices_of(i)]
-    meet([peer(dy, dx) for dy, dx in OFFSETS] + [partner, near[1], near[-1]])
-
-    for k in range(2):
+    pl.semaphore_wait(pltpu.get_barrier_semaphore(), len(friends))
+
+    for k in range(len(CHUNKS)):
         for dy, dx in OFFSETS:
             wires.send(("v", k, dy, dx), rotated.at[chunk(k)], full.at[y, x, core, chunk(k)], peer(dy, dx))
         wires.send(("p", k, 0, 0), rotated.at[chunk(k)], full.at[y, x, core, chunk(k)], partner)
@@ -179,42 +186,42 @@
         fetch(b).wait()
 
         def one(t, _):
-            value = stage[b % BUFFERS, t]
-            high, low = halves(value)
+            high, low = halves(stage[b % BUFFERS, t])
             tiles[b * BATCH + t, 0] = high
             tiles[b * BATCH + t, 1] = low
-            high, low = halves(jnp.transpose(value))
-            flipped[b * BATCH + t, 0] = high
-            flipped[b * BATCH + t, 1] = low
+            flipped[b * BATCH + t, 0] = jnp.transpose(high)
+            flipped[b * BATCH + t, 1] = jnp.transpose(low)
             return 0
 
-        lax.fori_loop(0, BATCH, one, 0, unroll=2)
+        lax.fori_loop(0, BATCH, one, 0, unroll=8)
         if b + BUFFERS < batches:
             fetch(b + BUFFERS).start()
 
-    def split_volume(k, yy, xx, c):
-        high, low = halves(full[yy, xx, c, chunk(k)])
+    def split_volume(k, value, yy, xx, c):
+        high, low = halves(value)
         at = (yy * NX + xx) * NC + c
-        sides[k, at, 0:HALF] = high
-        sides[k, at, HALF : 2 * HALF] = low
+        sides[k][at, 0 : length(k)] = high
+        sides[k][at, length(k) : 2 * length(k)] = low
 
     def receive_volume(k):
         for dy, dx in OFFSETS:
-            ref = full.at[turn(y, -dy, NY), turn(x, -dx, NX), core, chunk(k)]
+            yy, xx = turn(y, -dy, NY), turn(x, -dx, NX)
+            ref = full.at[yy, xx, core, chunk(k)]
             wires.wait(("v", k, dy, dx), ref, peer(-dy, -dx))
             wires.send(("p", k, dy, dx), ref, ref, partner)
-            split_volume(k, turn(y, -dy, NY), turn(x, -dx, NX), core)
+            split_volume(k, ref[...], yy, xx, core)
 
     def receive_partner(k):
         for dy, dx in [(0, 0)] + OFFSETS:
-            ref = full.at[turn(y, -dy, NY), turn(x, -dx, NX), 1 - core, chunk(k)]
+            yy, xx = turn(y, -dy, NY), turn(x, -dx, NX)
+            ref = full.at[yy, xx, 1 - core, chunk(k)]
             wires.wait(("p", k, dy, dx), ref, partner)
-            split_volume(k, turn(y, -dy, NY), turn(x, -dx, NX), 1 - core)
-
-    def products(row, shift, left, k, right, first, count):
+            split_volume(k, ref[...], yy, xx, 1 - core)
+
+    def products(row, shift, left, m, right, first, count):
         def some(g, _):
             at = first + g * UNROLL
-            running = sums[at]
+            running = sums[at, 0:m]
             before = lists[row, jnp.maximum(at - 1, 0)]
             for u in range(UNROLL):
                 entry = lists[row, at + u]
@@ -222,29 +229,31 @@
                 same = jnp.where(name == ((before >> shift) & 31), 1.0, 0.0)
                 operand = (entry >> (5 - shift)) & 31
                 t = within(entry >> 10, n_tiles)
-                both = dot(left[k, operand], right[t, 0])
-                value = both[0:HALF] + both[HALF : 2 * HALF] + dot(left[k, operand, 0:HALF], right[t, 1])
+                both = dot(left[operand], right[t, 0])
+                value = both[0:m] + both[m : 2 * m] + dot(left[operand, 0:m], right[t, 1])
                 running = value + running * same
-                sums[at + u + 1] = running
+                sums[at + u + 1, 0:m] = running
                 before = entry
             return 0
 
         lax.fori_loop(0, count // UNROLL, some, 0)
 
     def forward(k, first, count):
-        products(0, 5, sides, k, flipped, first, count)
+        products(0, 5, sides[k], length(k), flipped, first, count)
 
     def backward(k, first, count):
-        products(1, 0, back, k, tiles, first, count)
+        products(1, 0, back[k], length(k), tiles, first, count)
 
     def take_part(k):
+        place, number = CHUNKS[k]
+
         def one(j, _):
-            value = sums[within(lists[2, j], n_tiles + 1)]
-            for i in range(4):
-                part[4 * k + i, j] = value[i * WIDTH : (i + 1) * WIDTH]
+            at = within(lists[2, j], n_tiles + 1)
+            for i in range(number):
+                part[place + i, j] = sums[at, i * WIDTH : (i + 1) * WIDTH]
             return 0
 
-        lax.fori_loop(0, LIVE, one, 0, unroll=2)
+        lax.fori_loop(0, LIVE, one, 0, unroll=4)
 
     def weigh():
         look.wait()
@@ -255,7 +264,7 @@
             target[j] = jnp.log(BLANK / n)
             return 0
 
-        lax.fori_loop(0, LIVE, one, 0)
+        lax.fori_loop(0, LIVE, one, 0, unroll=2)
 
     size = LIVE // PIECES
     order = {1: list(range(PIECES)), -1: list(range(PIECES // 2, PIECES)) + list(range(PIECES // 2))}
@@ -281,9 +290,9 @@
             if not goes_far(way, i):
                 pass_on(way, 3, i, part.at[rel(3 * way), rows(i)])
 
-    def relay_sums(d):
+    def relay_sums(d, far):
         for way, i in pairs:
-            if d == 3 and not goes_far(way, i):
+            if goes_far(way, i) != far:
                 continue
             wires.wait(("r", way, d + 1, i), box(way, d + 1, i), near[-way])
             w = 0 if way == 1 else 1
@@ -307,85 +316,108 @@
                 deliver(way, 0, i)
             residual[rel(0), rows(i)] = value
 
-    def relay_residual(d):
-        for way, i in pairs:
-            if d == 4 and not goes_far(way, i):
+    def relay_residual(d, some=pairs, near_too=True):
+        for way, i in some:
+            if (d == 4 or not near_too) and not goes_far(way, i):
                 continue
             wires.wait(("g", way, d - 1, i), residual.at[rel(-d * way), rows(i)], near[-way])
             if d < 3 or (d == 3 and goes_far(way, i)):
                 deliver(way, d, i)
 
     def split_residual(k):
+        place, number = CHUNKS[k]
+
         def one(j, _):
-            for i in range(4):
-                high, low = halves(residual[4 * k + i, j])
-                back[k, j, i * WIDTH : (i + 1) * WIDTH] = high
-                back[k, j, HALF + i * WIDTH : HALF + (i + 1) * WIDTH] = low
+            for i in range(number):
+                high, low = halves(residual[place + i, j])
+                back[k][j, i * WIDTH : (i + 1) * WIDTH] = high
+                back[k][j, length(k) + i * WIDTH : length(k) + (i + 1) * WIDTH] = low
             return 0
 
-        lax.fori_loop(0, LIVE, one, 0, unroll=2)
+        lax.fori_loop(0, LIVE, one, 0, unroll=4)
 
     def start_grad(k):
-        for c in range(COLS):
-            grad[k, c // (NX * NC), (c // NC) % NX, c % NC] = sums[within(lists[3, c], n_tiles + 1)]
-        wires.send(("q", k), grad.at[k, :, :, 1 - core], mine.at[k], partner)
+        for dy in (2, 1, 3, 0):
+            yy = turn(y, dy, NY)
+            for n in range(NX * NC):
+                at = within(lists[3, yy * (NX * NC) + n], n_tiles + 1)
+                grad[yy, n // NC, n % NC, chunk(k)] = sums[at, 0 : length(k)]
+            wires.send(("q", k, dy), grad.at[yy, :, 1 - core, chunk(k)], mine.at[yy, :, chunk(k)], partner)
 
     def spread_grad(k):
-        wires.wait(("q", k), mine.at[k], partner)
-        for n, (dy, dx) in enumerate(OFFSETS):
-            yy, xx = turn(y, dy, NY), turn(x, dx, NX)
-            mine[k, yy, xx] += grad[k, yy, xx, core]
-            wires.send(("t", k, dy, dx), mine.at[k, yy, xx], terms.at[k, n], peer(dy, dx))
+        for dy in (2, 1, 3, 0):
+            yy = turn(y, dy, NY)
+            wires.wait(("q", k, dy), mine.at[yy, :, chunk(k)], partner)
+            for n, (to_y, dx) in enumerate(BY_ROW):
+                if to_y == dy:
+                    xx = turn(x, dx, NX)
+                    mine[yy, xx, chunk(k)] += grad[yy, xx, core, chunk(k)]
+                    wires.send(("t", k, n), mine.at[yy, xx, chunk(k)], terms.at[n, chunk(k)], peer(dy, dx))
 
     def finish_grad(k):
-        value = mine[k, y, x] + grad[k, y, x, core]
-        for n, (dy, dx) in enumerate(OFFSETS):
-            wires.wait(("t", k, dy, dx), terms.at[k, n], peer(-dy, -dx))
-            value = value + terms[k, n]
-        for i in range(4):
-            out[0, slices_of(4 * k + i)] = value[i * WIDTH : (i + 1) * WIDTH]
-
-    full[y, x, core] = rotated[...]
-    for k in range(2):
-        split_volume(k, y, x, core)
+        value = mine[y, x, chunk(k)] + grad[y, x, core, chunk(k)]
+        for n, (dy, dx) in enumerate(BY_ROW):
+            wires.wait(("t", k, n), terms.at[n, chunk(k)], peer(-dy, -dx))
+            value = value + terms[n, chunk(k)]
+        place, number = CHUNKS[k]
+        for i in range(number):
+            out[0, slices_of(place + i)] = value[i * WIDTH : (i + 1) * WIDTH]
+
+    quarter = n_tiles // 4
+    for k in range(len(CHUNKS)):
+        split_volume(k, rotated[chunk(k)], y, x, core)
+        for j in range(LIVE, 32):
+            back[k][j] = jnp.zeros(back[k].shape[1:], bf16)
     sums[0] = jnp.zeros(sums.shape[1:], f32)
-    for j in range(LIVE, 32):
-        back[0, j] = jnp.zeros(back.shape[2:], bf16)
-        back[1, j] = jnp.zeros(back.shape[2:], bf16)
-    for b in range(batches - 3):
+    for b in range(batches):
         prepare(b)
     receive_volume(0)
-    for b in range(batches - 3, batches):
-        prepare(b)
     give.wait()
     receive_partner(0)
-    quarter = n_tiles // 4
     forward(0, 0, n_tiles)
     take_part(0)
     start_sums()
     receive_volume(1)
+    weigh()
     receive_partner(1)
     forward(1, 0, 2 * quarter)
-    weigh()
-    relay_sums(3)
+    relay_sums(3, True)
+    receive_volume(2)
     forward(1, 2 * quarter, 2 * quarter)
     take_part(1)
-    relay_sums(2)
-    relay_sums(1)
+    relay_sums(2, False)
+    receive_partner(2)
+    forward(2, 0, quarter)
+    relay_sums(2, True)
+    forward(2, quarter, 3 * quarter)
+    take_part(2)
+    relay_sums(1, False)
+    relay_sums(1, True)
     finish_sums()
     relay_residual(1)
-    relay_residual(2)
+    split_residual(2)
+    backward(2, 0, quarter)
+    relay_residual(2, pairs[0:2])
+    relay_residual(2, pairs[2:4])
+    backward(2, quarter, quarter)
+    relay_residual(2, pairs[4:6])
+    backward(2, 2 * quarter, 2 * quarter)
+    relay_residual(2, pairs[6:8])
+    start_grad(2)
     split_residual(1)
+    relay_residual(3, pairs[0:4], near_too=False)
     backward(1, 0, 2 * quarter)
-    relay_residual(3)
+    spread_grad(2)
     backward(1, 2 * quarter, 2 * quarter)
     start_grad(1)
+    relay_residual(3, pairs[4:8])
     relay_residual(4)
     split_residual(0)
     backward(0, 0, quarter)
     spread_grad(1)
     backward(0, quarter, 3 * quarter)
     start_grad(0)
+    finish_grad(2)
     finish_grad(1)
     spread_grad(0)
     finish_grad(0)
@@ -395,7 +427,8 @@
 def shards(volume, projector, tile_ids, counts, ray_counts):
     n_tiles, rays, lanes = projector.shape
     slices = volume.shape[1]
-    n_sems = 2 * (2 * len(OFFSETS) + 1) + 4 * (PIECES // 2 + 3 * PIECES) + 2 * (len(OFFSETS) + 1)
+    n_sems = len(CHUNKS) * (3 * len(OFFSETS) + 1 + NY) + 4 * (PIECES // 2 + 3 * PIECES)
+    lengths = [number * WIDTH for _, number in CHUNKS]
     gradient = pl.pallas_call(
         step_kernel,
         out_shape=jax.ShapeDtypeStruct(volume.shape, f32),
@@ -407,9 +440,9 @@
             pltpu.VMEM((BUFFERS, BATCH, rays, lanes), f32),
             pltpu.VMEM((n_tiles, 2, rays, lanes), bf16),
             pltpu.VMEM((n_tiles, 2, lanes, rays), bf16),
-            pltpu.VMEM((2, COLS, 2 * HALF, lanes), bf16),
-            pltpu.VMEM((2, 32, 2 * HALF, rays), bf16),
-            pltpu.VMEM((n_tiles + 1, HALF, lanes), f32),
+            *[pltpu.VMEM((COLS, 2 * m, lanes), bf16) for m in lengths],
+            *[pltpu.VMEM((32, 2 * m, rays), bf16) for m in lengths],
+            pltpu.VMEM((n_tiles + 1, max(lengths), lanes), f32),
             pltpu.VMEM((NP, LIVE, WIDTH, rays), f32),
             pltpu.VMEM((2, 4, LIVE, WIDTH, rays), f32),
             pltpu.VMEM((LIVE, WIDTH, rays), f32),
@@ -417,9 +450,9 @@
             pltpu.VMEM((NP, LIVE, WIDTH, rays), f32),
             pltpu.VMEM((LIVE, WIDTH, rays), f32),
             pltpu.VMEM((counts.shape[0], WIDTH, rays), i32),
-            pltpu.VMEM((2, NY, NX, NC, HALF, lanes), f32),
-            pltpu.VMEM((2, NY, NX, HALF, lanes), f32),
-            pltpu.VMEM((2, len(OFFSETS), HALF, lanes), f32),
+            pltpu.VMEM((NY, NX, NC, slices, lanes), f32),
+            pltpu.VMEM((NY, NX, slices, lanes), f32),
+            pltpu.VMEM((len(OFFSETS), slices, lanes), f32),
             pltpu.VMEM((8, LANES), i32),
             pltpu.VMEM((8, LANES), i32),
             pltpu.SMEM((8, LANES), i32),

time: 85.9 us -> 74.4 us (0.87)
  Pallas kernels: 84.1 us -> 72.3 us
    pallas_call x1, Pallas kernels: 84.1 us -> 72.3 us  [shards(): pl.pallas_call(step_kernel, out_shape=jax.ShapeDtypeStruct(volume.shape,...]
where the time goes in v3:
time: 74.4 us; the launch traced here: 73.8 us
  Pallas kernels  72.3 us (97%)
  other arithmetic  1.48 us (2%)
    pallas_call x1, Pallas kernels, shards(): pl.pallas_call(step_kernel, out_shape=jax.ShapeDtypeStruct(volume.shape,...  72.3 us

profile of v3, /device:TPU:1, one launch (start us, length us, event | category | flops | bytes accessed | tf_op | source)
XLA Modules:
  0.0 73.8 jit_solution(17525071855023041286)
XLA Ops:
  0.0 0.0 copy-start
  0.0 72.3 %step.1 = f32[1,128,128]{2,1,0:T(8,128)} custom-call(s32[1,160]{1,0:T(1,128)} %bitcast.1, s32[1,8]{1,0:T(1,128)} %ray_counts.1, f32[1,128,128]{2,1,0:T(8,128)} %vol.1, f32[160,128,128]{2,1,0:T(8,128)} %projector.1, s32[32,128,128]{2,1,0:T(8,128)} %counts.1), custom_call_target="tpu_custom_call" | custom-call | tf_op jit(solution)/shard_map/step/pallas_call | solution.py:432
  72.3 0.0 copy-done
  72.3 1.5 %multiply_subtract_fusion = f32[1,128,128]{2,1,0:T(8,128)} fusion(f32[1,128,128]{2,1,0:T(8,128)S(1)} %copy-done, f32[1,128,128]{2,1,0:T(8,128)} %step.1), kind=kLoop, calls=%fused_computation | loop fusion | flops 32768 | bytes 196608 | tf_op jit(solution)/shard_map/sub | solution.py:469
Async XLA Ops:
  0.0 72.3 %copy-start = (f32[1,128,128]{2,1,0:T(8,128)S(1)}, f32[1,128,128]{2,1,0:T(8,128)}, u32[]{:S(2)}) copy-start(f32[1,128,128]{2,1,0:T(8,128)} %vol.1) | copy-start | bytes 196612

commit v4 on v3

--- a/solution.py
+++ b/solution.py
@@ -417,9 +417,9 @@
     spread_grad(1)
     backward(0, quarter, 3 * quarter)
     start_grad(0)
+    spread_grad(0)
     finish_grad(2)
     finish_grad(1)
-    spread_grad(0)
     finish_grad(0)
     wires.drain()
 

time: 74.4 us -> 73.8 us (level)
  no operation moved by 1% of the time
where the time goes in v4:
time: 73.8 us; the launch traced here: 73.6 us
  Pallas kernels  72.1 us (98%)
  other arithmetic  1.48 us (2%)
    pallas_call x1, Pallas kernels, shards(): pl.pallas_call(step_kernel, out_shape=jax.ShapeDtypeStruct(volume.shape,...  72.1 us
    sub x1, other arithmetic, shards(): return volume - STEP * gradient  1.48 us

profile of v4, /device:TPU:1, one launch (start us, length us, event | category | flops | bytes accessed | tf_op | source)
XLA Modules:
  0.0 73.6 jit_solution(982744673451314335)
XLA Ops:
  0.0 0.0 copy-start
  0.0 72.1 %step.1 = f32[1,128,128]{2,1,0:T(8,128)} custom-call(s32[1,160]{1,0:T(1,128)} %bitcast.1, s32[1,8]{1,0:T(1,128)} %ray_counts.1, f32[1,128,128]{2,1,0:T(8,128)} %vol.1, f32[160,128,128]{2,1,0:T(8,128)} %projector.1, s32[32,128,128]{2,1,0:T(8,128)} %counts.1), custom_call_target="tpu_custom_call" | custom-call | tf_op jit(solution)/shard_map/step/pallas_call | solution.py:432
  72.1 0.0 copy-done
  72.1 1.5 %multiply_subtract_fusion = f32[1,128,128]{2,1,0:T(8,128)} fusion(f32[1,128,128]{2,1,0:T(8,128)S(1)} %copy-done, f32[1,128,128]{2,1,0:T(8,128)} %step.1), kind=kLoop, calls=%fused_computation | loop fusion | flops 32768 | bytes 196608 | tf_op jit(solution)/shard_map/sub | solution.py:469
Async XLA Ops:
  0.0 72.1 %copy-start = (f32[1,128,128]{2,1,0:T(8,128)S(1)}, f32[1,128,128]{2,1,0:T(8,128)}, u32[]{:S(2)}) copy-start(f32[1,128,128]{2,1,0:T(8,128)} %vol.1) | copy-start | bytes 196612
